TPU v7x, 256 devices: a whole 4x4x8 slice. The times are simulated.
256 devices in a mesh: frames: 16 (over z, core), mp: 16 (over y, x).
Axes of the slice: x: 4, y: 4, z: 8, core: 2. Of those that a mesh axis runs over, the one named last changes fastest.
Arguments:
- motion: bfloat16 [256, 25, 1024], P('frames', None, 'mp'), may hold values from -6 to 6
- adjacency: float32 [2, 25, 25], replicated, may hold values from -1.25 to 1.25
- w_bc: bfloat16 [2, 1024, 128], P(None, 'mp'), may hold values from -0.1875 to 0.1875
- decay: float32 [2, 256, 1024], P(None, 'frames', 'mp'), may hold values from 0.5 to 1, as said below
- skip: float32 [2, 1024], P(None, 'mp'), may hold values from 0.5 to 1.5
- w_out: bfloat16 [2, 1024, 1024], P(None, 'mp'), may hold values from -0.25 to 0.25
Outputs:
- encoded: float32 [256, 25, 1024], P('frames', None, 'mp')
Inputs may be any that keep to these rules, and one draw needn't show every extreme that they name: `decay`: each entry lies strictly between 0 and 1.
All inputs are finite; a program needn't handle non-finite values.
Results may differ from a plain program's by a relative error of at most 0.012.
Values may be sent and summed in bfloat16 or wider, within the bound.
A program may use at most 64 MiB of HBM per device.

v0:
```python
import jax
import jax.numpy as jnp
from jax import lax
from jax.sharding import PartitionSpec as P

ENCODER_LAYERS = 2


def entering(value, axis, join, neutral):
    count, mine = (lax.axis_size(axis), lax.axis_index(axis))
    pieces = jax.tree.map(lambda part: lax.all_gather(part, axis), value)
    so_far = jax.tree.map(
        lambda part, zero: jnp.full_like(part, 0) + jnp.asarray(zero, part.dtype), value, neutral
    )

    def lap(position, so_far):
        longer = join(so_far, jax.tree.map(lambda part: part[position], pieces))
        return jax.tree.map(lambda new, old: jnp.where(position < mine, new, old), longer, so_far)

    return lax.fori_loop(0, count - 1, lap, so_far)


def shards(motion, adjacency, w_bc, decay, skip, w_out):
    highest = lax.Precision.HIGHEST
    frames_loc, joints, width_loc = motion.shape
    state = w_bc.shape[2] // 2
    x = motion.astype(jnp.float32)
    for layer in range(ENCODER_LAYERS):
        mixed = jnp.einsum("jk,tkd->tjd", adjacency[layer], x, precision=highest).astype(
            jnp.bfloat16
        )
        partial_coef = jnp.dot(
            mixed.reshape(-1, width_loc), w_bc[layer], preferred_element_type=jnp.float32
        )
        coef = lax.psum(partial_coef, "mp").reshape(frames_loc, joints, 2 * state)
        in_b = coef[:, :, :state]
        out_c = coef[:, :, state:]
        decay_speed = decay[layer]
        logs = jnp.cumsum(jnp.log(decay_speed), axis=0)
        upto = jnp.exp(logs)
        weighted = (
            (1.0 - decay_speed)[:, None, :] * mixed.astype(jnp.float32) * jnp.exp(-logs)[:, None, :]
        )
        later = lax.broadcasted_iota(jnp.int32, (frames_loc, frames_loc), 0)
        earlier = lax.broadcasted_iota(jnp.int32, (frames_loc, frames_loc), 1)
        grid = jnp.einsum("tjn,sjn->jts", out_c, in_b, precision=highest)
        grid = jnp.where((earlier <= later)[None], grid, 0.0)
        inner = upto[:, None, :] * jnp.einsum("jts,sjd->tjd", grid, weighted, precision=highest)
        total = upto[-1]
        end_state = jnp.einsum(
            "sjd,sjn->jdn", weighted * total[None, None, :], in_b, precision=highest
        )

        def link(first, second):
            return (first[0] * second[0], second[0][None, :, None] * first[1] + second[1])

        _, incoming = entering(
            (total, end_state), "frames", link, (jnp.ones_like(total), jnp.zeros_like(end_state))
        )
        outer = upto[:, None, :] * jnp.einsum("tjn,jdn->tjd", out_c, incoming, precision=highest)
        result = (inner + outer + skip[layer][None, None, :] * mixed.astype(jnp.float32)).astype(
            jnp.bfloat16
        )
        flat = result.reshape(-1, width_loc)
        weights = w_out[layer]
        summed = lax.psum_scatter(
            lax.dot_general(
                weights, flat, (((0,), (1,)), ((), ())), preferred_element_type=jnp.float32
            ),
            "mp",
            scatter_dimension=0,
            tiled=True,
        )
        update = summed.T.reshape(frames_loc, joints, width_loc)
        x = x + update
    return x


def solution(mesh):
    return jax.shard_map(
        shards,
        mesh=mesh,
        in_specs=(
            P("frames", None, "mp"),
            P(),
            P(None, "mp", None),
            P(None, "frames", "mp"),
            P(None, "mp"),
            P(None, "mp", None),
        ),
        out_specs=P("frames", None, "mp"),
        check_vma=False,
    )
```

profile of v0, /device:TPU:32, one launch (start us, length us, event | category | flops | bytes accessed | tf_op | source)
XLA Modules:
  0.0 580.5 jit_solution(17792508891115939289)
XLA Ops:
  7.4 1.2 fusion.36
  10.6 96.9 %all-reduce.3.cloned.1.call-done = f32[16,25,128]{2,0,1:T(8,128)} async-done(((f32[16,25,128]{2,0,1:T(8,128)}), f32[16,25,128]{2,0,1:T(8,128)}) %all-reduce.3.cloned.1.call-update) | async-done | bytes 204816 | tf_op jit(solution)/shard_map/psum | solution.py:35
  107.5 3.4 fusion.13
  111.0 15.9 %all-gather.2 = f32[16,1,64]{2,1,0:T(1,128)S(1)} all-gather(f32[1,1,64]{2,1,0:T(1,128)S(1)} %get-tuple-element.264), channel_id=1, replica_groups=mesh['frames'=16,'mp'=16] {'frames'}, dimensions={0}, use_global_device_ids=true | all-gather | bytes 4352 | tf_op jit(solution)/shard_map/all_gather | solution.py:11
  127.5 58.7 %all-gather.7.cloned.1.call-done = f32[400,64,64]{2,1,0:T(8,128)} async-done(((f32[25,64,64]{2,1,0:T(8,128)}), f32[400,64,64]{2,1,0:T(8,128)}) %all-gather.7.cloned.1.call-update) | async-done | bytes 6553616 | tf_op jit(solution)/shard_map/all_gather | solution.py:11
  186.2 21.0 %while.28 = (s32[]{:T(128)}, f32[25,64,64]{2,1,0:T(8,128)S(1)}, s32[]{:T(128)}, f32[16,64]{1,0:T(8,128)S(1)}, f32[16,25,64,64]{3,2,1,0:T(8,128)}, /*index=5*/s32[]{:T(128)}, s32[]{:T(128)}) while((s32[]{:T(128)}, f32[25,64,64]{2,1,0:T(8,128)S(1)}, s32[]{:T(128)}, f32[16,64]{1,0:T(8,128)S(1)}, f32[16,25,64,64]{3,2,1,0:T(8,128)}, ...), condition=%wide.region_3.4_spmd.clone, body=%wide.region_2.3_spmd.clone.sunk | while | flops 409604 | bytes 1229673 | solution.py:20
  186.2 1.4 fusion.68
  187.6 1.4 fusion.68
  189.0 1.4 fusion.68
  190.4 1.4 fusion.68
  191.8 1.4 fusion.68
  193.2 1.4 fusion.68
  194.6 1.4 fusion.68
  196.0 1.4 fusion.68
  197.4 1.4 fusion.68
  198.8 1.4 fusion.68
  200.2 1.4 fusion.68
  201.6 1.4 fusion.68
  203.0 1.4 fusion.68
  204.4 1.4 fusion.68
  205.8 1.4 fusion.68
  207.2 1.4 fusion.27
  209.5 1.8 copy.66
  211.4 79.9 %reduce-scatter.7.cloned.1.call-done = f32[64,400]{1,0:T(8,128)} async-done(((f32[1024,400]{1,0:T(8,128)}), f32[64,400]{1,0:T(8,128)}) %reduce-scatter.7.cloned.1.call-update) | async-done | bytes 102416
  294.0 94.0 %all-reduce.5.cloned.1.call-done = f32[16,25,128]{2,0,1:T(8,128)} async-done(((f32[16,25,128]{2,0,1:T(8,128)}), f32[16,25,128]{2,0,1:T(8,128)}) %all-reduce.5.cloned.1.call-update) | async-done | bytes 204816 | tf_op jit(solution)/shard_map/psum | solution.py:35
  387.9 3.4 fusion.18
  391.4 15.9 %all-gather.3 = f32[16,1,64]{2,1,0:T(1,128)S(1)} all-gather(f32[1,1,64]{2,1,0:T(1,128)S(1)} %get-tuple-element.260), channel_id=1, replica_groups=mesh['frames'=16,'mp'=16] {'frames'}, dimensions={0}, use_global_device_ids=true | all-gather | bytes 4352 | tf_op jit(solution)/shard_map/all_gather | solution.py:11
  407.8 58.8 %all-gather.9.cloned.1.call-done = f32[400,64,64]{2,1,0:T(8,128)} async-done(((f32[25,64,64]{2,1,0:T(8,128)}), f32[400,64,64]{2,1,0:T(8,128)}) %all-gather.9.cloned.1.call-update) | async-done | bytes 6553616 | tf_op jit(solution)/shard_map/all_gather | solution.py:11
  466.6 21.0 %while.29 = (s32[]{:T(128)}, f32[25,64,64]{2,1,0:T(8,128)S(1)}, s32[]{:T(128)}, f32[16,64]{1,0:T(8,128)S(1)}, f32[16,25,64,64]{3,2,1,0:T(8,128)}, /*index=5*/s32[]{:T(128)}, s32[]{:T(128)}) while((s32[]{:T(128)}, f32[25,64,64]{2,1,0:T(8,128)S(1)}, s32[]{:T(128)}, f32[16,64]{1,0:T(8,128)S(1)}, f32[16,25,64,64]{3,2,1,0:T(8,128)}, ...), condition=%wide.region_8.9_spmd.clone, body=%wide.region_7.8_spmd.clone.sunk | while | flops 409604 | bytes 1229673 | solution.py:20
  466.6 1.4 fusion.69
  468.0 1.4 fusion.69
  469.4 1.4 fusion.69
  470.8 1.4 fusion.69
  472.2 1.4 fusion.69
  473.6 1.4 fusion.69
  475.0 1.4 fusion.69
  476.4 1.4 fusion.69
  477.8 1.4 fusion.69
  479.2 1.4 fusion.69
  480.6 1.4 fusion.69
  482.0 1.4 fusion.69
  483.4 1.4 fusion.69
  484.8 1.4 fusion.69
  486.2 1.4 fusion.69
  487.6 1.4 fusion.22
  489.9 1.8 copy.68
  491.7 80.0 %reduce-scatter.9.cloned.1.call-done = f32[64,400]{1,0:T(8,128)} async-done(((f32[1024,400]{1,0:T(8,128)}), f32[64,400]{1,0:T(8,128)}) %reduce-scatter.9.cloned.1.call-update) | async-done | bytes 102416
  571.7 1.0 copy.69
  (96 shorter events, 9.5 us)
Async XLA Ops:
  6.5 4.0 copy-start.5
  6.5 101.0 %all-reduce.3.cloned.1.call-start = ((), (), s32[]{:S(2)}) async-start(), calls=%async_computation.2 | async-start | bytes 409600 | tf_op jit(solution)/shard_map/psum | solution.py:35
  8.5 118.4 %copy-start.6 = (f32[2,64]{1,0:T(2,128)S(1)}, f32[2,64]{1,0:T(2,128)}, u32[]{:S(2)}) copy-start(f32[2,64]{1,0:T(2,128)} %param.14) | copy-start | bytes 1540
  10.5 175.7 %all-gather.7.cloned.1.call-start = ((), (), s32[]{:S(2)}) async-start(), calls=%async_computation.4 | async-start | bytes 13926400 | tf_op jit(solution)/shard_map/all_gather | solution.py:11
  107.5 19.4 %copy-start = (f32[16,25,128]{2,0,1:T(8,128)S(1)}, f32[16,25,128]{2,0,1:T(8,128)}, u32[]{:S(2)}) copy-start(f32[16,25,128]{2,0,1:T(8,128)} %all-reduce.3.cloned.1.call-done) | copy-start | bytes 614404
  110.9 180.3 %reduce-scatter.7.cloned.1.call-start = ((), (), s32[]{:S(2)}) async-start(), calls=%async_computation.6 | async-start | bytes 2228224
  207.2 1.9 copy-start.3
  211.3 81.0 %copy-start.2 = (bf16[16,25,64]{2,0,1:T(8,128)(2,1)S(1)}, bf16[16,25,64]{2,0,1:T(8,128)(2,1)}, u32[]{:S(2)}) copy-start(bf16[16,25,64]{2,0,1:T(8,128)(2,1)} %param.10) | copy-start | bytes 153604
  211.3 81.6 %copy-start.4 = (bf16[2,64,128]{2,1,0:T(8,128)(2,1)S(1)}, bf16[2,64,128]{2,1,0:T(8,128)(2,1)}, u32[]{:S(2)}) copy-start(bf16[2,64,128]{2,1,0:T(8,128)(2,1)} %param.12) | copy-start | bytes 98308
  211.3 176.6 %all-reduce.5.cloned.1.call-start = ((), (), s32[]{:S(2)}) async-start(), calls=%async_computation.3 | async-start | bytes 409600 | tf_op jit(solution)/shard_map/psum | solution.py:35
  293.9 172.7 %all-gather.9.cloned.1.call-start = ((), (), s32[]{:S(2)}) async-start(), calls=%async_computation.5 | async-start | bytes 13926400 | tf_op jit(solution)/shard_map/all_gather | solution.py:11
  387.9 19.4 %copy-start.1 = (f32[16,25,128]{2,0,1:T(8,128)S(1)}, f32[16,25,128]{2,0,1:T(8,128)}, u32[]{:S(2)}) copy-start(f32[16,25,128]{2,0,1:T(8,128)} %all-reduce.5.cloned.1.call-done) | copy-start | bytes 614404
  391.3 180.4 %reduce-scatter.9.cloned.1.call-start = ((), (), s32[]{:S(2)}) async-start(), calls=%async_computation.7 | async-start | bytes 2228224
Sparse Core Ops, SparseCore 0:
  10.6 96.8 all-reduce.2
  111.0 75.0 all-gather.6
  211.4 79.7 reduce-scatter.6
  294.3 93.5 all-reduce.4
  391.4 75.0 all-gather.8
  491.8 79.8 reduce-scatter.8
where the time goes:
time: 582 us; the launch traced here: 580 us
  waiting for transfers between devices  468 us (80%)
  other arithmetic  40.9 us (7%)
  blocking collectives  31.9 us (5%)
  matrix products  14.6 us (3%)
  between operations  13.8 us (2%)
  local copies, waits for them, and re-layouts  9.76 us (2%)
    psum x2, waiting for transfers between devices, shards(): coef = lax.psum(partial_coef, 'mp').reshape(frames_loc, joints, 2 * state)  191 us
    unnamed x8, waiting for transfers between devices  160 us
    all_gather x2, waiting for transfers between devices, entering(): pieces = jax.tree.map(lambda part: lax.all_gather(part, axis), value)  117 us
    select_n x30, other arithmetic, lap(): jnp.where(position < mine, new, old)  40.7 us
    all_gather x2, blocking collectives, entering(): pieces = jax.tree.map(lambda part: lax.all_gather(part, axis), value)  31.9 us
  transfers between devices with their start and end apart: 6, of which 6 were waited for; matrix products, arithmetic and copies ran while one was open for 0% of the time, Pallas kernels for 0%

commit v1 on v0

--- a/solution.py
+++ b/solution.py
@@ -1,9 +1,19 @@
+import functools
 import jax
 import jax.numpy as jnp
 from jax import lax
 from jax.sharding import PartitionSpec as P
+from jax.lax import all_gather
 
 ENCODER_LAYERS = 2
+
+
+def search_cube(message, axis_name):
+    carry = jnp.sum(all_gather(message, axis_name=axis_name), 0)
+    return carry
+
+
+_turn_layers_all = functools.partial(search_cube, axis_name="mp")
 
 
 def entering(value, axis, join, neutral):
@@ -32,7 +42,7 @@
         partial_coef = jnp.dot(
             mixed.reshape(-1, width_loc), w_bc[layer], preferred_element_type=jnp.float32
         )
-        coef = lax.psum(partial_coef, "mp").reshape(frames_loc, joints, 2 * state)
+        coef = _turn_layers_all(partial_coef).reshape(frames_loc, joints, 2 * state)
         in_b = coef[:, :, :state]
         out_c = coef[:, :, state:]
         decay_speed = decay[layer]

time: 582 us -> 502 us (0.86)
  waiting for transfers between devices: 468 us -> 385 us
    psum x2 -> x0, waiting for transfers between devices: 191 us -> none  [shards(): coef = lax.psum(partial_coef, 'mp').reshape(frames_loc, joints, 2 * state)]
    all_gather x0 -> x2, waiting for transfers between devices: none -> 108 us  [search_cube(): carry = jnp.sum(all_gather(message, axis_name=axis_name), 0)]
where the time goes in v1:
time: 502 us; the launch traced here: 501 us
  waiting for transfers between devices  385 us (77%)
  other arithmetic  45.9 us (9%)
  blocking collectives  31.9 us (6%)
  matrix products  14.4 us (3%)
  between operations  13.8 us (3%)
  local copies, waits for them, and re-layouts  8.4 us (2%)
    unnamed x8, waiting for transfers between devices  160 us
    all_gather x2, waiting for transfers between devices, entering(): pieces = jax.tree.map(lambda part: lax.all_gather(part, axis), value)  117 us
    all_gather x2, waiting for transfers between devices, search_cube(): carry = jnp.sum(all_gather(message, axis_name=axis_name), 0)  108 us
    select_n x30, other arithmetic, lap(): jnp.where(position < mine, new, old)  40.8 us
    all_gather x2, blocking collectives, entering(): pieces = jax.tree.map(lambda part: lax.all_gather(part, axis), value)  31.9 us
  transfers between devices with their start and end apart: 6, of which 6 were waited for; matrix products, arithmetic and copies ran while one was open for 0% of the time, Pallas kernels for 0%

profile of v1, /device:TPU:32, one launch (start us, length us, event | category | flops | bytes accessed | tf_op | source)
XLA Modules:
  0.0 500.7 jit_solution(2690077143369318330)
XLA Ops:
  8.7 1.6 fusion.53
  11.1 55.3 %all-gather.11.cloned.1.call-done = f32[6400,128]{1,0:T(8,128)} async-done(((f32[400,128]{1,0:T(8,128)}), f32[6400,128]{1,0:T(8,128)}) %all-gather.11.cloned.1.call-update) | async-done | bytes 3276816 | tf_op jit(solution)/shard_map/all_gather | solution.py:12
  66.5 2.1 reduce_sum.18
  68.7 2.4 fusion.13
  71.2 15.9 %all-gather.4 = f32[16,1,64]{2,1,0:T(1,128)S(1)} all-gather(f32[1,1,64]{2,1,0:T(1,128)S(1)} %get-tuple-element.268), channel_id=1, replica_groups=mesh['frames'=16,'mp'=16] {'frames'}, dimensions={0}, use_global_device_ids=true | all-gather | bytes 4352 | tf_op jit(solution)/shard_map/all_gather | solution.py:21
  87.8 58.5 %all-gather.13.cloned.1.call-done = f32[400,64,64]{2,1,0:T(8,128)} async-done(((f32[25,64,64]{2,1,0:T(8,128)}), f32[400,64,64]{2,1,0:T(8,128)}) %all-gather.13.cloned.1.call-update) | async-done | bytes 6553616 | tf_op jit(solution)/shard_map/all_gather | solution.py:21
  146.4 21.1 %while.28 = (s32[]{:T(128)}, f32[25,64,64]{2,1,0:T(8,128)S(1)}, s32[]{:T(128)}, f32[16,64]{1,0:T(8,128)S(1)}, f32[16,25,64,64]{3,2,1,0:T(8,128)}, /*index=5*/s32[]{:T(128)}, s32[]{:T(128)}) while((s32[]{:T(128)}, f32[25,64,64]{2,1,0:T(8,128)S(1)}, s32[]{:T(128)}, f32[16,64]{1,0:T(8,128)S(1)}, f32[16,25,64,64]{3,2,1,0:T(8,128)}, ...), condition=%wide.region_3.4_spmd.clone, body=%wide.region_2.3_spmd.clone.sunk | while | flops 409604 | bytes 1229673 | solution.py:30
  146.4 1.4 fusion.70
  147.8 1.4 fusion.70
  149.2 1.4 fusion.70
  150.6 1.4 fusion.70
  152.0 1.4 fusion.70
  153.4 1.4 fusion.70
  154.9 1.4 fusion.70
  156.3 1.4 fusion.70
  157.7 1.4 fusion.70
  159.1 1.4 fusion.70
  160.5 1.4 fusion.70
  161.9 1.4 fusion.70
  163.3 1.4 fusion.70
  164.7 1.4 fusion.70
  166.1 1.4 fusion.70
  167.5 1.4 fusion.29
  169.7 1.8 copy.70
  171.6 79.9 %reduce-scatter.7.cloned.1.call-done = f32[64,400]{1,0:T(8,128)} async-done(((f32[1024,400]{1,0:T(8,128)}), f32[64,400]{1,0:T(8,128)}) %reduce-scatter.7.cloned.1.call-update) | async-done | bytes 102416
  254.1 52.8 %all-gather.15.cloned.1.call-done = f32[6400,128]{1,0:T(8,128)} async-done(((f32[400,128]{1,0:T(8,128)}), f32[6400,128]{1,0:T(8,128)}) %all-gather.15.cloned.1.call-update) | async-done | bytes 3276816 | tf_op jit(solution)/shard_map/all_gather | solution.py:12
  306.9 2.1 reduce_sum.19
  309.2 2.4 fusion.18
  311.6 15.9 %all-gather.5 = f32[16,1,64]{2,1,0:T(1,128)S(1)} all-gather(f32[1,1,64]{2,1,0:T(1,128)S(1)} %get-tuple-element.264), channel_id=1, replica_groups=mesh['frames'=16,'mp'=16] {'frames'}, dimensions={0}, use_global_device_ids=true | all-gather | bytes 4352 | tf_op jit(solution)/shard_map/all_gather | solution.py:21
  328.2 58.6 %all-gather.17.cloned.1.call-done = f32[400,64,64]{2,1,0:T(8,128)} async-done(((f32[25,64,64]{2,1,0:T(8,128)}), f32[400,64,64]{2,1,0:T(8,128)}) %all-gather.17.cloned.1.call-update) | async-done | bytes 6553616 | tf_op jit(solution)/shard_map/all_gather | solution.py:21
  386.8 21.0 %while.29 = (s32[]{:T(128)}, f32[25,64,64]{2,1,0:T(8,128)S(1)}, s32[]{:T(128)}, f32[16,64]{1,0:T(8,128)S(1)}, f32[16,25,64,64]{3,2,1,0:T(8,128)}, /*index=5*/s32[]{:T(128)}, s32[]{:T(128)}) while((s32[]{:T(128)}, f32[25,64,64]{2,1,0:T(8,128)S(1)}, s32[]{:T(128)}, f32[16,64]{1,0:T(8,128)S(1)}, f32[16,25,64,64]{3,2,1,0:T(8,128)}, ...), condition=%wide.region_8.9_spmd.clone, body=%wide.region_7.8_spmd.clone.sunk | while | flops 409604 | bytes 1229673 | solution.py:30
  388.2 1.4 fusion.71
  389.6 1.4 fusion.71
  391.0 1.4 fusion.71
  392.4 1.4 fusion.71
  393.8 1.4 fusion.71
  395.2 1.4 fusion.71
  396.6 1.4 fusion.71
  398.1 1.4 fusion.71
  399.5 1.4 fusion.71
  400.9 1.4 fusion.71
  402.3 1.4 fusion.71
  403.7 1.4 fusion.71
  405.1 1.4 fusion.71
  406.5 1.4 fusion.71
  407.8 1.4 fusion.24
  410.1 1.8 copy.72
  411.9 80.0 %reduce-scatter.9.cloned.1.call-done = f32[64,400]{1,0:T(8,128)} async-done(((f32[1024,400]{1,0:T(8,128)}), f32[64,400]{1,0:T(8,128)}) %reduce-scatter.9.cloned.1.call-update) | async-done | bytes 102416
  (92 shorter events, 12.5 us)
Async XLA Ops:
  6.5 59.9 %all-gather.11.cloned.1.call-start = ((), (), s32[]{:S(2)}) async-start(), calls=%async_computation.2 | async-start | bytes 3481600 | tf_op jit(solution)/shard_map/all_gather | solution.py:12
  10.3 136.1 %all-gather.13.cloned.1.call-start = ((), (), s32[]{:S(2)}) async-start(), calls=%async_computation.3 | async-start | bytes 13926400 | tf_op jit(solution)/shard_map/all_gather | solution.py:21
  66.5 20.7 %copy-start.3 = (f32[2,64]{1,0:T(2,128)S(1)}, f32[2,64]{1,0:T(2,128)}, u32[]{:S(2)}) copy-start(f32[2,64]{1,0:T(2,128)} %param.14) | copy-start | bytes 1540
  71.1 180.4 %reduce-scatter.7.cloned.1.call-start = ((), (), s32[]{:S(2)}) async-start(), calls=%async_computation.6 | async-start | bytes 2228224
  146.4 23.0 %copy-start.1 = (bf16[2,64,1024]{2,1,0:T(8,128)(2,1)S(1)}, bf16[2,64,1024]{2,1,0:T(8,128)(2,1)}, u32[]{:S(2)}) copy-start(bf16[2,64,1024]{2,1,0:T(8,128)(2,1)} %param.15) | copy-start | bytes 786436
  169.7 82.8 %copy-start = (bf16[16,25,64]{2,0,1:T(8,128)(2,1)S(1)}, bf16[16,25,64]{2,0,1:T(8,128)(2,1)}, u32[]{:S(2)}) copy-start(bf16[16,25,64]{2,0,1:T(8,128)(2,1)} %param.10) | copy-start | bytes 153604
  169.7 83.4 %copy-start.2 = (bf16[2,64,128]{2,1,0:T(8,128)(2,1)S(1)}, bf16[2,64,128]{2,1,0:T(8,128)(2,1)}, u32[]{:S(2)}) copy-start(bf16[2,64,128]{2,1,0:T(8,128)(2,1)} %param.12) | copy-start | bytes 98308
  171.6 135.3 %all-gather.15.cloned.1.call-start = ((), (), s32[]{:S(2)}) async-start(), calls=%async_computation.4 | async-start | bytes 3481600 | tf_op jit(solution)/shard_map/all_gather | solution.py:12
  254.0 132.8 %all-gather.17.cloned.1.call-start = ((), (), s32[]{:S(2)}) async-start(), calls=%async_computation.5 | async-start | bytes 13926400 | tf_op jit(solution)/shard_map/all_gather | solution.py:21
  311.6 180.3 %reduce-scatter.9.cloned.1.call-start = ((), (), s32[]{:S(2)}) async-start(), calls=%async_computation.7 | async-start | bytes 2228224
Sparse Core Ops, SparseCore 0:
  10.4 56.0 all-gather.10
  71.2 75.0 all-gather.12
  171.7 79.7 reduce-scatter.6
  254.1 52.7 all-gather.14
  311.7 75.0 all-gather.16
  412.1 79.7 reduce-scatter.8
